TPU v7x, 256 devices: a whole 4x4x8 slice. The times are simulated.
256 devices in a mesh: chan: 8 (over z), seqo: 4 (over y), seqi: 8 (over x, core).
Axes of the slice: x: 4, y: 4, z: 8, core: 2. Of those that a mesh axis runs over, the one named last changes fastest.
Arguments:
- gate_in: bfloat16 [65536, 4096], P(('seqo', 'seqi'), 'chan'), may hold values from -6 to 6
- value_in: bfloat16 [65536, 4096], P(('seqo', 'seqi'), 'chan'), may hold values from -6 to 6
- out_gate: bfloat16 [65536, 4096], P(('seqo', 'seqi'), 'chan'), may hold values from -6 to 6
- residual: bfloat16 [65536, 4096], P(('seqo', 'seqi'), 'chan'), may hold values from -200 to 200
- filters: bfloat16 [8, 32, 6, 65536], P('chan', ('seqo', 'seqi')), may hold values from -5 to 5
- kept_index: int32 [8, 128], P('chan'), may hold values from -1 to 511, as said below
- kept_owner: int32 [8, 128], P('chan'), may hold values from -1 to 31, as said below
- skip_bias: float32 [4096], P('chan'), may hold values from -1 to 1
- norm_gain: float32 [4096], P('chan'), may hold values from 0.5 to 1.5
Outputs:
- hidden_out: bfloat16 [65536, 4096], P(('seqo', 'seqi'), 'chan')
- normed: bfloat16 [65536, 4096], P(('seqo', 'seqi'), 'chan')
Inputs may be any that keep to these rules, and one draw needn't show every extreme that they name: `kept_index`: row s lists the kept channels of slab s in rising order, distinct, between 64 and 128 of them, followed by -1 in the unused slots; some slab lists exactly 128. `kept_owner`: -1 exactly where kept_index is -1, else a device index along seqo+seqi. Within a slab no device owns more than 6 kept channels, and in every slab some device owns exactly 6.
All inputs are finite; a program needn't handle non-finite values.
Results may differ from a plain program's by a relative error of at most 0.005.
Values may be sent and summed in bfloat16 or wider, within the bound.
A program may use at most 128 MiB of HBM per device.

v0:
```python
import jax
import jax.numpy as jnp
from jax import lax
from jax.sharding import PartitionSpec as P

FA = 512
norm_eps = 1e-06
highest = lax.Precision.HIGHEST


def owner_ranks(owners_row):
    is_live = owners_row >= 0
    slot_count = owners_row.shape[0]
    token_position = jnp.arange(slot_count, dtype=jnp.int32)
    earlier = (
        (owners_row[:, None] == owners_row[None, :])
        & is_live[None, :]
        & (token_position[None, :] < token_position[:, None])
    )
    return jnp.sum(earlier.astype(jnp.int32), axis=1)


def angle_table(first, second, modulus):
    product = first[:, None] * second[None, :] % modulus
    return 2.0 * jnp.pi / modulus * product.astype(jnp.float32)


def causal_convolve(signals, kernels, outer_len):
    channels, length = signals.shape
    inner_len = 2 * length // outer_len
    total_len = outer_len * inner_len
    outer_steps = jnp.arange(outer_len, dtype=jnp.int32)
    half_steps = jnp.arange(outer_len // 2, dtype=jnp.int32)
    inner_steps = jnp.arange(inner_len, dtype=jnp.int32)
    outer_angle = angle_table(outer_steps, half_steps, outer_len)
    twist_angle = angle_table(outer_steps, inner_steps, total_len)
    inner_angle = angle_table(inner_steps, inner_steps, inner_len)
    outer_cos = jnp.cos(outer_angle)
    outer_sin = jnp.sin(outer_angle)
    twist_cos = jnp.cos(twist_angle)
    twist_sin = jnp.sin(twist_angle)
    inner_cos = jnp.cos(inner_angle)
    inner_sin = jnp.sin(inner_angle)
    outer_fwd = jnp.concatenate([outer_cos, -outer_sin], axis=0)
    inner_fwd = jnp.concatenate(
        [
            jnp.concatenate([inner_cos, -inner_sin], axis=1),
            jnp.concatenate([inner_sin, inner_cos], axis=1),
        ],
        axis=0,
    )
    inner_back = jnp.concatenate(
        [
            jnp.concatenate([inner_cos, inner_sin], axis=1),
            jnp.concatenate([-inner_sin, inner_cos], axis=1),
        ],
        axis=0,
    )
    outer_back = jnp.concatenate([outer_cos, -outer_sin], axis=0)

    def forward(series):
        blocks = series.astype(jnp.float32).reshape(channels, outer_len // 2, inner_len)
        first = jnp.einsum("ka,cab->ckb", outer_fwd, blocks, precision=highest)
        first_re = first[:, :outer_len]
        first_im = first[:, outer_len:]
        turned_re = first_re * twist_cos + first_im * twist_sin
        turned_im = first_im * twist_cos - first_re * twist_sin
        stacked = jnp.concatenate([turned_re, turned_im], axis=2)
        spec = jnp.einsum("ckb,bj->ckj", stacked, inner_fwd, precision=highest)
        return (spec[:, :, :inner_len], spec[:, :, inner_len:])

    signal_re, signal_im = forward(signals)
    kernel_re, kernel_im = forward(kernels)
    joint_re = signal_re * kernel_re - signal_im * kernel_im
    joint_im = signal_re * kernel_im + signal_im * kernel_re
    joint = jnp.concatenate([joint_re, joint_im], axis=2)
    back = jnp.einsum("ckj,jb->ckb", joint, inner_back, precision=highest)
    back_re = back[:, :, :inner_len]
    back_im = back[:, :, inner_len:]
    untwist_re = back_re * twist_cos - back_im * twist_sin
    untwist_im = back_im * twist_cos + back_re * twist_sin
    untwisted = jnp.concatenate([untwist_re, untwist_im], axis=1)
    result = jnp.einsum("ka,ckb->cab", outer_back, untwisted, precision=highest)
    return (result / total_len).reshape(channels, length)


def local(
    gate_in, value_in, out_gate, residual, filters, kept_index, kept_owner, skip_bias, norm_gain
):
    tok_rows, slab_width = gate_in.shape
    own_slots = filters.shape[2]
    length = filters.shape[3]
    outer_devices = lax.axis_size("seqo")
    inner_devices = lax.axis_size("seqi")
    owner_count = outer_devices * inner_devices
    gated_prod = (gate_in.astype(jnp.float32) * value_in.astype(jnp.float32)).astype(jnp.bfloat16)
    index_row = kept_index[0]
    owners_row = kept_owner[0]
    is_live = owners_row >= 0
    slot_ranks = owner_ranks(owners_row)
    target = jnp.where(is_live, slot_ranks * owner_count + owners_row, -1)
    buffer_rows = jnp.arange(own_slots * owner_count, dtype=jnp.int32)
    select = (buffer_rows[:, None] == target[None, :]).astype(jnp.bfloat16)
    channel_pos = jnp.arange(slab_width, dtype=jnp.int32)
    spread = ((index_row[:, None] == channel_pos[None, :]) & is_live[:, None]).astype(jnp.bfloat16)
    picker = jnp.dot(select, spread, preferred_element_type=jnp.float32).astype(jnp.bfloat16)
    outgoing = lax.dot_general(
        picker, gated_prod, (((1,), (1,)), ((), ())), preferred_element_type=jnp.float32
    ).astype(jnp.bfloat16)
    incoming = lax.all_to_all(
        outgoing.reshape(own_slots, owner_count, tok_rows),
        ("seqo", "seqi"),
        split_axis=1,
        concat_axis=1,
        tiled=True,
    )
    convolved = causal_convolve(incoming.reshape(own_slots, length), filters[0, 0], FA)
    returned = lax.all_to_all(
        convolved.reshape(own_slots, owner_count, tok_rows),
        ("seqo", "seqi"),
        split_axis=1,
        concat_axis=1,
        tiled=True,
    )
    returned = returned.reshape(own_slots * owner_count, tok_rows)
    safe_target = jnp.where(is_live, target, 0)
    kept_rows = jnp.take(returned, safe_target, axis=0)
    put_at = jnp.where(is_live, index_row, slab_width)
    conv_cols = (
        jnp.zeros((tok_rows, slab_width), jnp.float32).at[:, put_at].set(kept_rows.T, mode="drop")
    )
    gated_wide = gated_prod.astype(jnp.float32)
    mixed_out = out_gate.astype(jnp.float32) * (conv_cols + skip_bias[None, :] * gated_wide)
    hidden_out = (residual.astype(jnp.float32) + mixed_out).astype(jnp.bfloat16)
    hidden_wide = hidden_out.astype(jnp.float32)
    squares = jnp.sum(hidden_wide * hidden_wide, axis=1)
    row_total = lax.psum(squares, "chan")
    width_all = slab_width * lax.axis_size("chan")
    scaling = lax.rsqrt(row_total / width_all + norm_eps)
    normed = (hidden_wide * scaling[:, None] * norm_gain[None, :]).astype(jnp.bfloat16)
    return (hidden_out, normed)


def solution(mesh):
    in_specs = (
        P(("seqo", "seqi"), "chan"),
        P(("seqo", "seqi"), "chan"),
        P(("seqo", "seqi"), "chan"),
        P(("seqo", "seqi"), "chan"),
        P("chan", ("seqo", "seqi"), None, None),
        P("chan", None),
        P("chan", None),
        P("chan"),
        P("chan"),
    )
    out_specs = (P(("seqo", "seqi"), "chan"), P(("seqo", "seqi"), "chan"))
    return jax.shard_map(local, mesh=mesh, in_specs=in_specs, out_specs=out_specs, check_vma=False)
```

profile of v0, /device:TPU:0, one launch (start us, length us, event | category | flops | bytes accessed | tf_op | source)
XLA Modules:
  0.0 187.8 jit_solution(6840904414468012201)
XLA Ops:
  3.5 2.9 %copy.66 = bf16[2048,512]{0,1:T(8,128)(2,1)S(1)} copy(bf16[2048,512]{1,0:T(8,128)(2,1)} %param.9) | data formatting | bytes 4194304 | tf_op args[0]
  6.5 4.6 %copy.67 = bf16[2048,512]{0,1:T(8,128)(2,1)} copy(bf16[2048,512]{1,0:T(8,128)(2,1)} %param.10) | data formatting | bytes 4194304 | tf_op args[1]
  11.1 2.5 %convolution_convert_fusion = bf16[192,2048]{1,0:T(8,128)(2,1)S(1)} fusion(bf16[2048,512]{0,1:T(8,128)(2,1)} %copy.67, bf16[2048,512]{0,1:T(8,128)(2,1)S(1)} %copy.66, s32[128]{0:T(128)S(1)} %bitcast.65, pred[128]{0:T(512)(128)(4,1)S(1)} %get-tuple-element.24, s32[128]{0:T(128)S(1)} %fusion.70), kind=kOutput, calls=%fused_computation.35 | convolution fusion | flops 432660480 | bytes 4981888 | tf_op jit(solution)/shard_map/dot_general | solution.py:107
  15.0 6.2 %all-to-all-start = ((bf16[6,32,2048]{2,0,1:T(8,128)(2,1)}), bf16[6,32,2048]{2,0,1:T(8,128)(2,1)}, u32[]{:S(2)}, u32[]{:S(2)}) async-start(bf16[6,32,2048]{2,0,1:T(8,128)(2,1)} %copy.68), calls=%async_computation | async-start | bytes 2097152 | tf_op jit(solution)/shard_map/all_to_all | solution.py:110
  21.2 1.9 %fusion.54 = f32[512,256]{1,0:T(8,128)S(1)} fusion(), kind=kLoop, calls=%fused_computation.83 | loop fusion | flops 1835008 | bytes 524288 | tf_op jit(solution)/shard_map/cos | solution.py:40
  23.1 1.9 %fusion.53 = f32[512,256]{1,0:T(8,128)S(1)} fusion(), kind=kLoop, calls=%fused_computation.82 | loop fusion | flops 1835008 | bytes 524288 | tf_op jit(solution)/shard_map/sin | solution.py:41
  28.0 1.8 fusion.60
  29.8 2.1 %sine_negate_fusion = (f32[512,256]{1,0:T(8,128)S(1)}, f32[512,256]{1,0:T(8,128)S(1)}) fusion(), kind=kLoop, calls=%fused_computation.64 | loop fusion | flops 1966080 | bytes 1048576 | tf_op jit(solution)/shard_map/neg | solution.py:44
  31.9 4.6 %convolution_bitcast_fusion = f32[6,1024,256]{1,2,0:T(8,128)} fusion(bf16[1,6,256,256]{3,1,2,0:T(8,128)(2,1)S(1)} %bitcast.63, f32[512,256]{1,0:T(8,128)S(1)} %get-tuple-element.26, f32[512,256]{1,0:T(8,128)S(1)} %get-tuple-element.27), kind=kOutput, calls=%fused_computation.33 | convolution fusion | flops 4832100352 | bytes 8126464 | tf_op jit(solution)/shard_map/ka,cab->ckb/dot_general | solution.py:63
  36.5 1.9 all-to-all-done
  38.4 2.7 %copy.69 = bf16[6,32,2048]{2,1,0:T(8,128)(2,1)} copy(bf16[6,32,2048]{2,0,1:T(8,128)(2,1)} %all-to-all-done) | data formatting | bytes 1572864 | tf_op jit(solution)/shard_map/all_to_all | solution.py:110
  41.0 2.8 %reshape.146 = bf16[6,256,256]{2,1,0:T(8,128)(2,1)} reshape(bf16[6,32,2048]{2,1,0:T(8,128)(2,1)} %copy.69) | data formatting | bytes 1572864 | tf_op jit(solution)/shard_map/reshape | solution.py:62
  43.9 4.8 %convolution_bitcast_fusion.1 = f32[6,1024,256]{1,2,0:T(8,128)S(1)} fusion(bf16[6,256,256]{2,1,0:T(8,128)(2,1)} %reshape.146, f32[512,256]{1,0:T(8,128)S(1)} %get-tuple-element.26, f32[512,256]{1,0:T(8,128)S(1)} %get-tuple-element.27), kind=kOutput, calls=%fused_computation.34 | convolution fusion | flops 4832100352 | bytes 8126464 | tf_op jit(solution)/shard_map/ka,cab->ckb/dot_general | solution.py:63
  48.8 2.9 %multiply_add_fusion.3 = (f32[6,512,256]{1,2,0:T(8,128)S(1)}, f32[6,512,256]{1,2,0:T(8,128)S(1)}, f32[6,512,256]{1,2,0:T(8,128)S(1)}, f32[6,512,256]{1,2,0:T(8,128)}) fusion(f32[6,1024,256]{1,2,0:T(8,128)S(1)} %convolution_bitcast_fusion.1, f32[512,256]{0,1:T(8,128)S(1)} %copy-done.8, f32[512,256]{0,1:T(8,128)S(1)} %copy-done.6, f32[6,1024,256]{1,2,0:T(8,128)S(1)} %bitcast.60), kind=kLoop, calls=%fused_computation.32 | loop fusion | flops 9437184 | bytes 26214400 | tf_op jit(solution)/shard_map/add | solution.py:66
  51.7 12.5 %fusion = f32[6,512,512]{1,2,0:T(8,128)S(1)} fusion(f32[6,512,256]{1,2,0:T(8,128)S(1)} %get-tuple-element.17, f32[6,512,256]{1,2,0:T(8,128)S(1)} %get-tuple-element.16, f32[256,256]{0,1:T(8,128)S(1)} %copy-done.12, f32[256,256]{0,1:T(8,128)S(1)} %copy-done.11, f32[256,256]{0,1:T(8,128)S(1)} %fusion.66), kind=kOutput, calls=%fused_computation.2 | convolution fusion | flops 9666035712 | bytes 13369344 | tf_op jit(solution)/shard_map/ckb,bj->ckj/dot_general | solution.py:69
  64.2 12.8 %fusion.4 = f32[6,512,512]{1,2,0:T(8,128)S(1)} fusion(f32[6,512,256]{1,2,0:T(8,128)S(1)} %get-tuple-element.20, f32[6,512,256]{1,2,0:T(8,128)S(1)} %copy-done.3, f32[256,256]{0,1:T(8,128)S(1)} %copy-done.12, f32[256,256]{0,1:T(8,128)S(1)} %copy-done.11, f32[256,256]{0,1:T(8,128)S(1)} %fusion.66), kind=kOutput, calls=%fused_computation.6 | convolution fusion | flops 9666035712 | bytes 13369344 | tf_op jit(solution)/shard_map/ckb,bj->ckj/dot_general | solution.py:69
  77.0 1.6 multiply_subtract_fusion.1
  78.6 14.0 %fusion.8 = f32[6,512,512]{1,2,0:T(8,128)S(1)} fusion(f32[6,512,256]{1,2,0:T(8,128)S(1)} %get-tuple-element.13, f32[6,512,256]{1,2,0:T(8,128)S(1)} %get-tuple-element.12, f32[256,256]{0,1:T(8,128)} %get-tuple-element.29, f32[256,256]{0,1:T(8,128)} %copy-done.10, f32[256,256]{0,1:T(8,128)} %get-tuple-element.28), kind=kOutput, calls=%fused_computation.10 | convolution fusion | flops 9666035712 | bytes 13369344 | tf_op jit(solution)/shard_map/ckj,jb->ckb/dot_general | solution.py:77
  93.7 6.7 %multiply_bitcast_fusion = f32[6,256,256]{1,2,0:T(8,128)} fusion(f32[6,512,256]{1,2,0:T(8,128)S(1)} %get-tuple-element.15, f32[6,512,256]{1,2,0:T(8,128)S(1)} %get-tuple-element.14, f32[512,256]{1,0:T(8,128)S(1)} %get-tuple-element.26, f32[512,256]{1,0:T(8,128)S(1)} %copy-done.5), kind=kOutput, calls=%fused_computation.38 | convolution fusion | flops 4834066432 | bytes 8912896 | tf_op jit(solution)/shard_map/ka,ckb->cab/dot_general | solution.py:83
  100.4 1.9 copy.80
  102.5 2.3 %copy.81 = f32[6,32,2048]{2,0,1:T(8,128)} copy(f32[6,32,2048]{2,1,0:T(8,128)S(1)} %reshape_reshape.3) | data formatting | bytes 3145728 | tf_op jit(solution)/shard_map/reshape;reshape | solution.py:119
  104.8 5.6 %all-to-all-start.1 = ((f32[6,32,2048]{2,0,1:T(8,128)}), f32[6,32,2048]{2,0,1:T(8,128)S(1)}, u32[]{:S(2)}, u32[]{:S(2)}) async-start(f32[6,32,2048]{2,0,1:T(8,128)} %copy.81), calls=%async_computation.1 | async-start | bytes 4194304 | tf_op jit(solution)/shard_map/all_to_all | solution.py:118
  110.4 4.0 %copy.64 = bf16[2048,512]{0,1:T(8,128)(2,1)} copy(bf16[2048,512]{1,0:T(8,128)(2,1)} %param.12) | data formatting | bytes 4194304 | tf_op args[3]
  114.4 4.0 %copy.65 = bf16[2048,512]{0,1:T(8,128)(2,1)} copy(bf16[2048,512]{1,0:T(8,128)(2,1)} %param.11) | data formatting | bytes 4194304 | tf_op args[2]
  118.4 22.1 %all-to-all-done.1 = f32[6,32,2048]{2,0,1:T(8,128)S(1)} async-done(((f32[6,32,2048]{2,0,1:T(8,128)}), f32[6,32,2048]{2,0,1:T(8,128)S(1)}, u32[]{:S(2)}, u32[]{:S(2)}) %all-to-all-start.1) | async-done | bytes 1572896 | tf_op jit(solution)/shard_map/all_to_all | solution.py:118
  140.5 2.1 %copy.82 = f32[6,32,2048]{2,1,0:T(8,128)} copy(f32[6,32,2048]{2,0,1:T(8,128)S(1)} %all-to-all-done.1) | data formatting | bytes 3145728 | tf_op jit(solution)/shard_map/all_to_all | solution.py:118
  142.6 6.2 %scatter_custom_fusion = f32[2048,512]{0,1:T(8,128)} fusion(s32[128]{0:T(128)S(1)} %get-tuple-element.23, f32[]{:T(128)} %constant.60.clone.1, f32[]{:T(128)} %constant.76.clone.1, pred[128]{0:T(512)(128)(4,1)S(1)} %get-tuple-element.25, f32[192,2048]{1,0:T(8,128)} %bitcast.61, s32[1024]{0:T(1024)S(1)} %pad_clamp_fusion), kind=kCustom, calls=%fused_computation.36 | custom fusion | flops 262144 | bytes 5771784 | tf_op jit(solution)/shard_map/scatter | solution.py:130
  148.8 7.6 %fusion.16 = (f32[2048]{0:T(1024)S(1)}, bf16[2048,512]{0,1:T(8,128)(2,1)}) fusion(f32[2048,512]{0,1:T(8,128)} %scatter_custom_fusion, bf16[2048,512]{0,1:T(8,128)(2,1)} %copy.67, bf16[2048,512]{0,1:T(8,128)(2,1)S(1)} %copy-done.1, f32[512]{0:T(512)S(1)} %copy-done.15, bf16[2048,512]{0,1:T(8,128)(2,1)} %copy.65, bf16[2048,512]{0,1:T(8,128)(2,1)} %copy.64), kind=kLoop, calls=%fused_computation.20 | loop fusion | flops 15726592 | bytes 14690304 | tf_op jit(solution)/shard_map/reduce_sum | solution.py:136
  156.4 21.4 %psum.7 = f32[2048]{0:T(1024)S(1)} all-reduce(f32[2048]{0:T(1024)S(1)} %get-tuple-element.10), channel_id=1, replica_groups=mesh['chan'=8,'seqo'=4,'seqi'=8] {'chan'}, use_global_device_ids=true, to_apply=%region_3.4 | all-reduce | flops 2048 | bytes 16384 | tf_op jit(solution)/shard_map/psum | solution.py:137
  177.9 3.9 %copy.83 = bf16[2048,512]{1,0:T(8,128)(2,1)} copy(bf16[2048,512]{0,1:T(8,128)(2,1)} %get-tuple-element.11) | data formatting | bytes 4194304
  181.8 1.8 fusion.18
  183.7 3.9 %copy.84 = bf16[2048,512]{1,0:T(8,128)(2,1)} copy(bf16[2048,512]{0,1:T(8,128)(2,1)} %fusion.18) | data formatting | bytes 4194304
  (54 shorter events, 8.7 us)
Async XLA Ops:
  6.5 7.1 %copy-start = (bf16[2048,512]{0,1:T(8,128)(2,1)}, bf16[2048,512]{0,1:T(8,128)(2,1)S(1)}, u32[]{:S(2)}) copy-start(bf16[2048,512]{0,1:T(8,128)(2,1)S(1)} %copy.66) | copy-start | bytes 6291460
  6.5 4.6 %copy-start.17 = (s32[1,128]{1,0:T(1,128)S(1)}, s32[1,128]{1,0:T(1,128)}, u32[]{:S(2)}) copy-start(s32[1,128]{1,0:T(1,128)} %param.14) | copy-start | bytes 1540
  15.0 16.9 %copy-start.13 = (bf16[1,1,6,65536]{3,2,1,0:T(8,128)(2,1)S(1)}, bf16[1,1,6,65536]{3,2,1,0:T(8,128)(2,1)}, u32[]{:S(2)}) copy-start(bf16[1,1,6,65536]{3,2,1,0:T(8,128)(2,1)} %param.13) | copy-start | bytes 2359300
  15.0 23.4 %all-to-all-start = ((bf16[6,32,2048]{2,0,1:T(8,128)(2,1)}), bf16[6,32,2048]{2,0,1:T(8,128)(2,1)}, u32[]{:S(2)}, u32[]{:S(2)}) async-start(bf16[6,32,2048]{2,0,1:T(8,128)(2,1)} %copy.68), calls=%async_computation | async-start | bytes 2097152 | tf_op jit(solution)/shard_map/all_to_all | solution.py:110
  28.0 36.2 %copy-start.10 = (f32[256,256]{0,1:T(8,128)}, f32[256,256]{0,1:T(8,128)S(1)}, u32[]{:S(2)}) copy-start(f32[256,256]{0,1:T(8,128)S(1)} %fusion.66) | copy-start | bytes 786436
  31.8 12.0 %copy-start.4 = (f32[512,256]{1,0:T(8,128)}, f32[512,256]{1,0:T(8,128)S(1)}, u32[]{:S(2)}) copy-start(f32[512,256]{1,0:T(8,128)S(1)} %get-tuple-element.27) | copy-start | bytes 1572868
  38.3 10.4 %slice-start = ((s8[6291456]{0:T(1024)(128)(4,1)}), s8[2097152]{0:T(1024)(128)(4,1)S(1)}, s32[]{:S(2)}) async-start(s8[6291456]{0:T(1024)(128)(4,1)} %bitcast.59), calls=%async_computation.2 | async-start | bytes 4194304
  43.9 4.9 %slice-start.1 = ((s8[6291456]{0:T(1024)(128)(4,1)}), s8[4194304]{0:T(1024)(128)(4,1)S(1)}, s32[]{:S(2)}) async-start(s8[6291456]{0:T(1024)(128)(4,1)} %bitcast.59), calls=%async_computation.3 | async-start | bytes 8388608
  43.9 4.9 %copy-start.6 = (f32[512,256]{0,1:T(8,128)S(1)}, f32[512,256]{0,1:T(8,128)}, u32[]{:S(2)}) copy-start(f32[512,256]{0,1:T(8,128)} %copy.71) | copy-start | bytes 1572868
  43.9 4.9 %copy-start.8 = (f32[512,256]{0,1:T(8,128)S(1)}, f32[512,256]{0,1:T(8,128)}, u32[]{:S(2)}) copy-start(f32[512,256]{0,1:T(8,128)} %copy.72) | copy-start | bytes 1572868
  48.8 2.9 %copy-start.11 = (f32[256,256]{0,1:T(8,128)S(1)}, f32[256,256]{0,1:T(8,128)}, u32[]{:S(2)}) copy-start(f32[256,256]{0,1:T(8,128)} %get-tuple-element.28) | copy-start | bytes 786436
  48.8 2.9 %copy-start.12 = (f32[256,256]{0,1:T(8,128)S(1)}, f32[256,256]{0,1:T(8,128)}, u32[]{:S(2)}) copy-start(f32[256,256]{0,1:T(8,128)} %get-tuple-element.29) | copy-start | bytes 786436
  51.7 12.5 %copy-start.3 = (f32[6,512,256]{1,2,0:T(8,128)S(1)}, f32[6,512,256]{1,2,0:T(8,128)}, u32[]{:S(2)}) copy-start(f32[6,512,256]{1,2,0:T(8,128)} %get-tuple-element.21) | copy-start | bytes 9437188
  78.6 14.0 %copy-start.7 = (f32[512,256]{0,1:T(8,128)S(1)}, f32[512,256]{0,1:T(8,128)}, u32[]{:S(2)}) copy-start(f32[512,256]{0,1:T(8,128)} %copy.71) | copy-start | bytes 1572868
  78.6 14.0 %copy-start.9 = (f32[512,256]{0,1:T(8,128)S(1)}, f32[512,256]{0,1:T(8,128)}, u32[]{:S(2)}) copy-start(f32[512,256]{0,1:T(8,128)} %copy.72) | copy-start | bytes 1572868
  92.6 1.0 copy-start.5
  104.8 35.7 %all-to-all-start.1 = ((f32[6,32,2048]{2,0,1:T(8,128)}), f32[6,32,2048]{2,0,1:T(8,128)S(1)}, u32[]{:S(2)}, u32[]{:S(2)}) async-start(f32[6,32,2048]{2,0,1:T(8,128)} %copy.81), calls=%async_computation.1 | async-start | bytes 4194304 | tf_op jit(solution)/shard_map/all_to_all | solution.py:118
  114.4 4.0 %copy-start.14 = (s32[1,128]{1,0:T(1,128)S(1)}, s32[1,128]{1,0:T(1,128)}, u32[]{:S(2)}) copy-start(s32[1,128]{1,0:T(1,128)} %param.15) | copy-start | bytes 1540
  142.6 6.2 %copy-start.1 = (bf16[2048,512]{0,1:T(8,128)(2,1)S(1)}, bf16[2048,512]{0,1:T(8,128)(2,1)}, u32[]{:S(2)}) copy-start(bf16[2048,512]{0,1:T(8,128)(2,1)} %copy-done) | copy-start | bytes 6291460
  142.6 6.2 %copy-start.15 = (f32[512]{0:T(512)S(1)}, f32[512]{0:T(512)}, u32[]{:S(2)}) copy-start(f32[512]{0:T(512)} %param.16) | copy-start | bytes 6148
  156.4 25.4 %copy-start.2 = (bf16[2048,512]{0,1:T(8,128)(2,1)S(1)}, bf16[2048,512]{0,1:T(8,128)(2,1)}, u32[]{:S(2)}) copy-start(bf16[2048,512]{0,1:T(8,128)(2,1)} %get-tuple-element.11) | copy-start | bytes 6291460
  156.4 25.4 %copy-start.16 = (f32[512]{0:T(512)S(1)}, f32[512]{0:T(512)}, u32[]{:S(2)}) copy-start(f32[512]{0:T(512)} %param.17) | copy-start | bytes 6148
where the time goes:
time: 191 us; the launch traced here: 188 us
  matrix products  57.9 us (30%)
  local copies, waits for them, and re-layouts  38.8 us (20%)
  other arithmetic  32.7 us (17%)
  waiting for transfers between devices  23.9 us (13%)
  blocking collectives  21.4 us (11%)
  starting transfers between devices  11.8 us (6%)
    dot_general x2, matrix products, forward(): spec = jnp.einsum('ckb,bj->ckj', stacked, inner_fwd, precision=highest)  25.3 us
    unnamed x46, local copies, waits for them, and re-layouts  23.4 us
    all_to_all x1, waiting for transfers between devices, local(): lax.all_to_all(convolved.reshape(own_slots, owner_count, tok_rows), ('seq...  22.1 us
    psum x1, blocking collectives, local(): row_total = lax.psum(squares, 'chan')  21.4 us
    dot_general x1, matrix products, causal_convolve(): back = jnp.einsum('ckj,jb->ckb', joint, inner_back, precision=highest)  14 us
    dot_general x2, matrix products, forward(): first = jnp.einsum('ka,cab->ckb', outer_fwd, blocks, precision=highest)  9.43 us
    reduce_sum x1, other arithmetic, local(): squares = jnp.sum(hidden_wide * hidden_wide, axis=1)  7.64 us
    dot_general x1, matrix products, causal_convolve(): result = jnp.einsum('ka,ckb->cab', outer_back, untwisted, precision=highest)  6.74 us
  transfers between devices with their start and end apart: 2, of which 2 were waited for; matrix products, arithmetic and copies ran while one was open for 12% of the time, Pallas kernels for 0%

commit v1 on v0

--- a/solution.py
+++ b/solution.py
@@ -134,7 +134,8 @@
     hidden_out = (residual.astype(jnp.float32) + mixed_out).astype(jnp.bfloat16)
     hidden_wide = hidden_out.astype(jnp.float32)
     squares = jnp.sum(hidden_wide * hidden_wide, axis=1)
-    row_total = lax.psum(squares, "chan")
+    all_values = lax.all_gather(squares, "chan")
+    row_total = jnp.sum(all_values, axis=0)
     width_all = slab_width * lax.axis_size("chan")
     scaling = lax.rsqrt(row_total / width_all + norm_eps)
     normed = (hidden_wide * scaling[:, None] * norm_gain[None, :]).astype(jnp.bfloat16)

time: 191 us -> 200 us (1.047)
  the two profiles are of different devices: /device:TPU:0 before, /device:TPU:32 now
where the time goes in v1:
time: 200 us; the launch traced here: 197 us
  matrix products  57.9 us (29%)
  local copies, waits for them, and re-layouts  38.8 us (19%)
  other arithmetic  34.1 us (17%)
  blocking collectives  27.2 us (14%)
  waiting for transfers between devices  24 us (12%)
  starting transfers between devices  13.5 us (7%)
    all_gather x1, blocking collectives, local(): all_values = lax.all_gather(squares, 'chan')  27.2 us
    dot_general x2, matrix products, forward(): spec = jnp.einsum('ckb,bj->ckj', stacked, inner_fwd, precision=highest)  25.3 us
    unnamed x46, local copies, waits for them, and re-layouts  23.4 us
    all_to_all x1, waiting for transfers between devices, local(): lax.all_to_all(convolved.reshape(own_slots, owner_count, tok_rows), ('seq...  22.1 us
    dot_general x1, matrix products, causal_convolve(): back = jnp.einsum('ckj,jb->ckb', joint, inner_back, precision=highest)  14 us
    dot_general x2, matrix products, forward(): first = jnp.einsum('ka,cab->ckb', outer_fwd, blocks, precision=highest)  9.42 us
    all_to_all x1, starting transfers between devices, local(): lax.all_to_all(outgoing.reshape(own_slots, owner_count, tok_rows), ('seqo...  7.88 us
    reduce_sum x1, other arithmetic, local(): squares = jnp.sum(hidden_wide * hidden_wide, axis=1)  7.64 us
  transfers between devices with their start and end apart: 2, of which 2 were waited for; matrix products, arithmetic and copies ran while one was open for 12% of the time, Pallas kernels for 0%

profile of v1, /device:TPU:32, one launch (start us, length us, event | category | flops | bytes accessed | tf_op | source)
XLA Modules:
  0.0 196.6 jit_solution(4543693357059099065)
XLA Ops:
  3.5 2.9 %copy.66 = bf16[2048,512]{0,1:T(8,128)(2,1)S(1)} copy(bf16[2048,512]{1,0:T(8,128)(2,1)} %param.9) | data formatting | bytes 4194304 | tf_op args[0]
  6.5 4.6 %copy.67 = bf16[2048,512]{0,1:T(8,128)(2,1)} copy(bf16[2048,512]{1,0:T(8,128)(2,1)} %param.10) | data formatting | bytes 4194304 | tf_op args[1]
  11.1 2.5 %convolution_convert_fusion = bf16[192,2048]{1,0:T(8,128)(2,1)S(1)} fusion(bf16[2048,512]{0,1:T(8,128)(2,1)} %copy.67, bf16[2048,512]{0,1:T(8,128)(2,1)S(1)} %copy.66, s32[128]{0:T(128)S(1)} %bitcast.65, pred[128]{0:T(512)(128)(4,1)S(1)} %get-tuple-element.24, s32[128]{0:T(128)S(1)} %fusion.70), kind=kOutput, calls=%fused_computation.35 | convolution fusion | flops 432660480 | bytes 4981888 | tf_op jit(solution)/shard_map/dot_general | solution.py:107
  15.0 7.9 %all-to-all-start = ((bf16[6,32,2048]{2,0,1:T(8,128)(2,1)}), bf16[6,32,2048]{2,0,1:T(8,128)(2,1)}, u32[]{:S(2)}, u32[]{:S(2)}) async-start(bf16[6,32,2048]{2,0,1:T(8,128)(2,1)} %copy.68), calls=%async_computation | async-start | bytes 2097152 | tf_op jit(solution)/shard_map/all_to_all | solution.py:110
  22.9 1.9 fusion.54
  24.8 1.9 fusion.53
  29.7 1.8 fusion.60
  31.5 2.1 %sine_negate_fusion = (f32[512,256]{1,0:T(8,128)S(1)}, f32[512,256]{1,0:T(8,128)S(1)}) fusion(), kind=kLoop, calls=%fused_computation.64 | loop fusion | flops 1966080 | bytes 1048576 | tf_op jit(solution)/shard_map/neg | solution.py:44
  33.6 4.6 %convolution_bitcast_fusion = f32[6,1024,256]{1,2,0:T(8,128)} fusion(bf16[1,6,256,256]{3,1,2,0:T(8,128)(2,1)S(1)} %bitcast.63, f32[512,256]{1,0:T(8,128)S(1)} %get-tuple-element.26, f32[512,256]{1,0:T(8,128)S(1)} %get-tuple-element.27), kind=kOutput, calls=%fused_computation.33 | convolution fusion | flops 4832100352 | bytes 8126464 | tf_op jit(solution)/shard_map/ka,cab->ckb/dot_general | solution.py:63
  38.2 1.9 all-to-all-done
  40.1 2.7 %copy.69 = bf16[6,32,2048]{2,1,0:T(8,128)(2,1)} copy(bf16[6,32,2048]{2,0,1:T(8,128)(2,1)} %all-to-all-done) | data formatting | bytes 1572864 | tf_op jit(solution)/shard_map/all_to_all | solution.py:110
  42.8 2.8 %reshape.150 = bf16[6,256,256]{2,1,0:T(8,128)(2,1)} reshape(bf16[6,32,2048]{2,1,0:T(8,128)(2,1)} %copy.69) | data formatting | bytes 1572864 | tf_op jit(solution)/shard_map/reshape | solution.py:62
  45.6 4.8 %convolution_bitcast_fusion.1 = f32[6,1024,256]{1,2,0:T(8,128)S(1)} fusion(bf16[6,256,256]{2,1,0:T(8,128)(2,1)} %reshape.150, f32[512,256]{1,0:T(8,128)S(1)} %get-tuple-element.26, f32[512,256]{1,0:T(8,128)S(1)} %get-tuple-element.27), kind=kOutput, calls=%fused_computation.34 | convolution fusion | flops 4832100352 | bytes 8126464 | tf_op jit(solution)/shard_map/ka,cab->ckb/dot_general | solution.py:63
  50.5 2.9 %multiply_add_fusion.3 = (f32[6,512,256]{1,2,0:T(8,128)S(1)}, f32[6,512,256]{1,2,0:T(8,128)S(1)}, f32[6,512,256]{1,2,0:T(8,128)S(1)}, f32[6,512,256]{1,2,0:T(8,128)}) fusion(f32[6,1024,256]{1,2,0:T(8,128)S(1)} %convolution_bitcast_fusion.1, f32[512,256]{0,1:T(8,128)S(1)} %copy-done.8, f32[512,256]{0,1:T(8,128)S(1)} %copy-done.6, f32[6,1024,256]{1,2,0:T(8,128)S(1)} %bitcast.60), kind=kLoop, calls=%fused_computation.32 | loop fusion | flops 9437184 | bytes 26214400 | tf_op jit(solution)/shard_map/add | solution.py:66
  53.4 12.5 %fusion = f32[6,512,512]{1,2,0:T(8,128)S(1)} fusion(f32[6,512,256]{1,2,0:T(8,128)S(1)} %get-tuple-element.17, f32[6,512,256]{1,2,0:T(8,128)S(1)} %get-tuple-element.16, f32[256,256]{0,1:T(8,128)S(1)} %copy-done.12, f32[256,256]{0,1:T(8,128)S(1)} %copy-done.11, f32[256,256]{0,1:T(8,128)S(1)} %fusion.66), kind=kOutput, calls=%fused_computation.2 | convolution fusion | flops 9666035712 | bytes 13369344 | tf_op jit(solution)/shard_map/ckb,bj->ckj/dot_general | solution.py:69
  65.9 12.8 %fusion.4 = f32[6,512,512]{1,2,0:T(8,128)S(1)} fusion(f32[6,512,256]{1,2,0:T(8,128)S(1)} %get-tuple-element.20, f32[6,512,256]{1,2,0:T(8,128)S(1)} %copy-done.3, f32[256,256]{0,1:T(8,128)S(1)} %copy-done.12, f32[256,256]{0,1:T(8,128)S(1)} %copy-done.11, f32[256,256]{0,1:T(8,128)S(1)} %fusion.66), kind=kOutput, calls=%fused_computation.6 | convolution fusion | flops 9666035712 | bytes 13369344 | tf_op jit(solution)/shard_map/ckb,bj->ckj/dot_general | solution.py:69
  78.7 1.6 multiply_subtract_fusion.1
  80.3 14.0 %fusion.8 = f32[6,512,512]{1,2,0:T(8,128)S(1)} fusion(f32[6,512,256]{1,2,0:T(8,128)S(1)} %get-tuple-element.13, f32[6,512,256]{1,2,0:T(8,128)S(1)} %get-tuple-element.12, f32[256,256]{0,1:T(8,128)} %get-tuple-element.29, f32[256,256]{0,1:T(8,128)} %copy-done.10, f32[256,256]{0,1:T(8,128)} %get-tuple-element.28), kind=kOutput, calls=%fused_computation.10 | convolution fusion | flops 9666035712 | bytes 13369344 | tf_op jit(solution)/shard_map/ckj,jb->ckb/dot_general | solution.py:77
  95.4 6.7 %multiply_bitcast_fusion = f32[6,256,256]{1,2,0:T(8,128)} fusion(f32[6,512,256]{1,2,0:T(8,128)S(1)} %get-tuple-element.15, f32[6,512,256]{1,2,0:T(8,128)S(1)} %get-tuple-element.14, f32[512,256]{1,0:T(8,128)S(1)} %get-tuple-element.26, f32[512,256]{1,0:T(8,128)S(1)} %copy-done.5), kind=kOutput, calls=%fused_computation.38 | convolution fusion | flops 4834066432 | bytes 8912896 | tf_op jit(solution)/shard_map/ka,ckb->cab/dot_general | solution.py:83
  102.1 1.9 copy.80
  104.2 2.3 %copy.81 = f32[6,32,2048]{2,0,1:T(8,128)} copy(f32[6,32,2048]{2,1,0:T(8,128)S(1)} %reshape_reshape.3) | data formatting | bytes 3145728 | tf_op jit(solution)/shard_map/reshape;reshape | solution.py:119
  106.5 5.6 %all-to-all-start.1 = ((f32[6,32,2048]{2,0,1:T(8,128)}), f32[6,32,2048]{2,0,1:T(8,128)S(1)}, u32[]{:S(2)}, u32[]{:S(2)}) async-start(f32[6,32,2048]{2,0,1:T(8,128)} %copy.81), calls=%async_computation.1 | async-start | bytes 4194304 | tf_op jit(solution)/shard_map/all_to_all | solution.py:118
  112.1 4.0 %copy.64 = bf16[2048,512]{0,1:T(8,128)(2,1)} copy(bf16[2048,512]{1,0:T(8,128)(2,1)} %param.12) | data formatting | bytes 4194304 | tf_op args[3]
  116.1 4.0 %copy.65 = bf16[2048,512]{0,1:T(8,128)(2,1)} copy(bf16[2048,512]{1,0:T(8,128)(2,1)} %param.11) | data formatting | bytes 4194304 | tf_op args[2]
  120.1 22.1 %all-to-all-done.1 = f32[6,32,2048]{2,0,1:T(8,128)S(1)} async-done(((f32[6,32,2048]{2,0,1:T(8,128)}), f32[6,32,2048]{2,0,1:T(8,128)S(1)}, u32[]{:S(2)}, u32[]{:S(2)}) %all-to-all-start.1) | async-done | bytes 1572896 | tf_op jit(solution)/shard_map/all_to_all | solution.py:118
  142.2 2.1 %copy.82 = f32[6,32,2048]{2,1,0:T(8,128)} copy(f32[6,32,2048]{2,0,1:T(8,128)S(1)} %all-to-all-done.1) | data formatting | bytes 3145728 | tf_op jit(solution)/shard_map/all_to_all | solution.py:118
  144.3 7.5 %scatter_custom_fusion = f32[2048,512]{0,1:T(8,128)} fusion(s32[128]{0:T(128)S(1)} %get-tuple-element.23, f32[]{:T(128)} %constant.60.clone.1, f32[]{:T(128)} %constant.76.clone.1, pred[128]{0:T(512)(128)(4,1)S(1)} %get-tuple-element.25, f32[192,2048]{1,0:T(8,128)} %bitcast.61, s32[1024]{0:T(1024)S(1)} %pad_clamp_fusion), kind=kCustom, calls=%fused_computation.36 | custom fusion | flops 262144 | bytes 5771784 | tf_op jit(solution)/shard_map/scatter | solution.py:130
  151.8 7.6 %fusion.16 = (f32[2048]{0:T(1024)S(1)}, bf16[2048,512]{0,1:T(8,128)(2,1)}) fusion(f32[2048,512]{0,1:T(8,128)} %scatter_custom_fusion, bf16[2048,512]{0,1:T(8,128)(2,1)} %copy.67, bf16[2048,512]{0,1:T(8,128)(2,1)S(1)} %copy-done.1, f32[512]{0:T(512)S(1)} %copy-done.15, bf16[2048,512]{0,1:T(8,128)(2,1)} %copy.65, bf16[2048,512]{0,1:T(8,128)(2,1)} %copy.64), kind=kLoop, calls=%fused_computation.20 | loop fusion | flops 15726592 | bytes 14690304 | tf_op jit(solution)/shard_map/reduce_sum | solution.py:136
  159.5 27.2 %all-gather = f32[16384]{0:T(1024)S(1)} all-gather(f32[2048]{0:T(1024)S(1)} %get-tuple-element.10), channel_id=2, replica_groups=mesh['chan'=8,'seqo'=4,'seqi'=8] {'chan'}, dimensions={0}, use_global_device_ids=true | all-gather | bytes 73728 | tf_op jit(solution)/shard_map/all_gather | solution.py:137
  186.7 3.9 %copy.83 = bf16[2048,512]{1,0:T(8,128)(2,1)} copy(bf16[2048,512]{0,1:T(8,128)(2,1)} %get-tuple-element.11) | data formatting | bytes 4194304
  190.6 1.8 fusion.18
  192.5 3.9 %copy.84 = bf16[2048,512]{1,0:T(8,128)(2,1)} copy(bf16[2048,512]{0,1:T(8,128)(2,1)} %fusion.18) | data formatting | bytes 4194304
  (56 shorter events, 8.7 us)
Async XLA Ops:
  6.5 7.1 %copy-start = (bf16[2048,512]{0,1:T(8,128)(2,1)}, bf16[2048,512]{0,1:T(8,128)(2,1)S(1)}, u32[]{:S(2)}) copy-start(bf16[2048,512]{0,1:T(8,128)(2,1)S(1)} %copy.66) | copy-start | bytes 6291460
  6.5 4.6 %copy-start.17 = (s32[1,128]{1,0:T(1,128)S(1)}, s32[1,128]{1,0:T(1,128)}, u32[]{:S(2)}) copy-start(s32[1,128]{1,0:T(1,128)} %param.14) | copy-start | bytes 1540
  15.0 18.6 %copy-start.13 = (bf16[1,1,6,65536]{3,2,1,0:T(8,128)(2,1)S(1)}, bf16[1,1,6,65536]{3,2,1,0:T(8,128)(2,1)}, u32[]{:S(2)}) copy-start(bf16[1,1,6,65536]{3,2,1,0:T(8,128)(2,1)} %param.13) | copy-start | bytes 2359300
  15.0 25.1 %all-to-all-start = ((bf16[6,32,2048]{2,0,1:T(8,128)(2,1)}), bf16[6,32,2048]{2,0,1:T(8,128)(2,1)}, u32[]{:S(2)}, u32[]{:S(2)}) async-start(bf16[6,32,2048]{2,0,1:T(8,128)(2,1)} %copy.68), calls=%async_computation | async-start | bytes 2097152 | tf_op jit(solution)/shard_map/all_to_all | solution.py:110
  29.7 36.2 %copy-start.10 = (f32[256,256]{0,1:T(8,128)}, f32[256,256]{0,1:T(8,128)S(1)}, u32[]{:S(2)}) copy-start(f32[256,256]{0,1:T(8,128)S(1)} %fusion.66) | copy-start | bytes 786436
  33.6 12.0 %copy-start.4 = (f32[512,256]{1,0:T(8,128)}, f32[512,256]{1,0:T(8,128)S(1)}, u32[]{:S(2)}) copy-start(f32[512,256]{1,0:T(8,128)S(1)} %get-tuple-element.27) | copy-start | bytes 1572868
  40.1 10.4 %slice-start = ((s8[6291456]{0:T(1024)(128)(4,1)}), s8[2097152]{0:T(1024)(128)(4,1)S(1)}, s32[]{:S(2)}) async-start(s8[6291456]{0:T(1024)(128)(4,1)} %bitcast.59), calls=%async_computation.2 | async-start | bytes 4194304
  45.6 4.9 %slice-start.1 = ((s8[6291456]{0:T(1024)(128)(4,1)}), s8[4194304]{0:T(1024)(128)(4,1)S(1)}, s32[]{:S(2)}) async-start(s8[6291456]{0:T(1024)(128)(4,1)} %bitcast.59), calls=%async_computation.3 | async-start | bytes 8388608
  45.6 4.9 %copy-start.6 = (f32[512,256]{0,1:T(8,128)S(1)}, f32[512,256]{0,1:T(8,128)}, u32[]{:S(2)}) copy-start(f32[512,256]{0,1:T(8,128)} %copy.71) | copy-start | bytes 1572868
  45.6 4.9 %copy-start.8 = (f32[512,256]{0,1:T(8,128)S(1)}, f32[512,256]{0,1:T(8,128)}, u32[]{:S(2)}) copy-start(f32[512,256]{0,1:T(8,128)} %copy.72) | copy-start | bytes 1572868
  50.5 2.9 %copy-start.11 = (f32[256,256]{0,1:T(8,128)S(1)}, f32[256,256]{0,1:T(8,128)}, u32[]{:S(2)}) copy-start(f32[256,256]{0,1:T(8,128)} %get-tuple-element.28) | copy-start | bytes 786436
  50.5 2.9 %copy-start.12 = (f32[256,256]{0,1:T(8,128)S(1)}, f32[256,256]{0,1:T(8,128)}, u32[]{:S(2)}) copy-start(f32[256,256]{0,1:T(8,128)} %get-tuple-element.29) | copy-start | bytes 786436
  53.4 12.5 %copy-start.3 = (f32[6,512,256]{1,2,0:T(8,128)S(1)}, f32[6,512,256]{1,2,0:T(8,128)}, u32[]{:S(2)}) copy-start(f32[6,512,256]{1,2,0:T(8,128)} %get-tuple-element.21) | copy-start | bytes 9437188
  80.3 14.0 %copy-start.7 = (f32[512,256]{0,1:T(8,128)S(1)}, f32[512,256]{0,1:T(8,128)}, u32[]{:S(2)}) copy-start(f32[512,256]{0,1:T(8,128)} %copy.71) | copy-start | bytes 1572868
  80.3 14.0 %copy-start.9 = (f32[512,256]{0,1:T(8,128)S(1)}, f32[512,256]{0,1:T(8,128)}, u32[]{:S(2)}) copy-start(f32[512,256]{0,1:T(8,128)} %copy.72) | copy-start | bytes 1572868
  94.3 1.0 copy-start.5
  106.5 35.7 %all-to-all-start.1 = ((f32[6,32,2048]{2,0,1:T(8,128)}), f32[6,32,2048]{2,0,1:T(8,128)S(1)}, u32[]{:S(2)}, u32[]{:S(2)}) async-start(f32[6,32,2048]{2,0,1:T(8,128)} %copy.81), calls=%async_computation.1 | async-start | bytes 4194304 | tf_op jit(solution)/shard_map/all_to_all | solution.py:118
  116.1 4.0 %copy-start.14 = (s32[1,128]{1,0:T(1,128)S(1)}, s32[1,128]{1,0:T(1,128)}, u32[]{:S(2)}) copy-start(s32[1,128]{1,0:T(1,128)} %param.15) | copy-start | bytes 1540
  144.3 7.5 %copy-start.1 = (bf16[2048,512]{0,1:T(8,128)(2,1)S(1)}, bf16[2048,512]{0,1:T(8,128)(2,1)}, u32[]{:S(2)}) copy-start(bf16[2048,512]{0,1:T(8,128)(2,1)} %copy-done) | copy-start | bytes 6291460
  144.3 7.6 %copy-start.15 = (f32[512]{0:T(512)S(1)}, f32[512]{0:T(512)}, u32[]{:S(2)}) copy-start(f32[512]{0:T(512)} %param.16) | copy-start | bytes 6148
  159.5 31.2 %copy-start.2 = (bf16[2048,512]{0,1:T(8,128)(2,1)S(1)}, bf16[2048,512]{0,1:T(8,128)(2,1)}, u32[]{:S(2)}) copy-start(bf16[2048,512]{0,1:T(8,128)(2,1)} %get-tuple-element.11) | copy-start | bytes 6291460
  159.5 31.2 %copy-start.16 = (f32[512]{0:T(512)S(1)}, f32[512]{0:T(512)}, u32[]{:S(2)}) copy-start(f32[512]{0:T(512)} %param.17) | copy-start | bytes 6148
